TPU v7x, 32 devices: a whole 2x2x4 slice. The times are simulated.
32 devices in a mesh: row: 2 (over y), col: 4 (over z), layer: 4 (over x, core).
Axes of the slice: x: 2, y: 2, z: 4, core: 2. Of those that a mesh axis runs over, the one named last changes fastest.
Arguments:
- eigvecs: float32 [16384, 8192], P('row', ('col', 'layer')), may hold values from -6 to 6
- first_vectors: float32 [16384, 128], P(('row', 'layer'), 'col'), may hold values from -0.375 to 0.375
- second_vectors: float32 [16384, 128], P(('row', 'layer'), 'col'), may hold values from -0.375 to 0.375
- first_factors: float32 [8192, 128], P(('row', 'layer'), 'col'), may hold values from -0.5 to 0.5
- second_factors: float32 [8192, 128], P(('row', 'layer'), 'col'), may hold values from -0.5 to 0.5
- panel_vectors: float32 [16384, 256], P(('row', 'layer')), may hold values from -0.125 to 0.125
- panel_factor: float32 [256, 256], replicated, may hold values from -0.375 to 0.375
Outputs:
- transformed: float32 [16384, 8192], P(('row', 'layer'), 'col')
All inputs are finite; a program needn't handle non-finite values.
Results may differ from a plain program's by a relative error of at most 0.000082.
Values sent between devices are 32-bit elements; how exact they have to be, the bound alone decides.
No kernel may reach another device: no remote copies, remote signals or barrier semaphores. Data moves between devices by JAX's collectives and lax.ppermute only.
A program may use at most 128 MiB of HBM per device.

v0:
```python
import jax
import jax.numpy as jnp
from jax import lax
from jax.sharding import PartitionSpec as P


def with_halo(array, sides, width):
    for axis, dim in sides:
        devices, length = (lax.axis_size(axis), array.shape[dim])
        up = [(i, (i + 1) % devices) for i in range(devices - 1)]
        down = [(j, i) for i, j in up]
        last = lax.slice_in_dim(array, length - width, length, axis=dim)
        first = lax.slice_in_dim(array, 0, width, axis=dim)
        before = lax.ppermute(last, axis, up)
        after = lax.ppermute(first, axis, down)
        array = jnp.concatenate([before, array, after], axis=dim)
    return array


def from_behind(value, axis, steps):
    count = lax.axis_size(axis)
    first, last = (max(0, -steps), min(count, count - steps))
    return lax.ppermute(value, axis, [(source, source + steps) for source in range(first, last)])


def apply_windows(data, vectors, factors):
    count = factors.shape[0] // 128
    width = data.shape[1]
    blocks = data.reshape(count, 256, width)
    vec_blocks = vectors.reshape(count, 256, 128)
    tri_blocks = jnp.triu(factors.reshape(count, 128, 128))
    proj = jnp.einsum("kri,krc->kic", vec_blocks, blocks, precision=lax.Precision.HIGHEST)
    scaled = jnp.einsum("kij,kjc->kic", tri_blocks, proj, precision=lax.Precision.HIGHEST)
    update = jnp.einsum("kri,kic->krc", vec_blocks, scaled, precision=lax.Precision.HIGHEST)
    return (blocks - update).reshape(count * 256, width)


def band_sweeps(data, vec_first, vec_second, fac_first, fac_second, extend, following):
    height = data.shape[0]
    width = data.shape[1]
    aligned = apply_windows(data, vec_first, fac_first)
    padded = extend(jnp.concatenate([aligned, vec_second], axis=1))
    next_factor = following(fac_second[:128])
    extended = jnp.concatenate([fac_second, next_factor], axis=0)
    offset = apply_windows(padded[:, :width], padded[:, width:], extended)
    return offset[128 : height + 128]


def band_tile(data, vec_first, vec_second, fac_first, fac_second):

    def extend(joined):
        return with_halo(joined, ((("row", "layer"), 0),), 128)

    def following(factor):
        return from_behind(factor, ("row", "layer"), -1)

    return band_sweeps(data, vec_first, vec_second, fac_first, fac_second, extend, following)


def to_tiles(data):
    return lax.all_to_all(data, "layer", split_axis=0, concat_axis=1, tiled=True)


def panel_tile(data, panel_vectors, upper):
    partial_value = jnp.dot(
        panel_vectors.T, data, precision=lax.Precision.HIGHEST, preferred_element_type=jnp.float32
    )
    projection = lax.psum(partial_value, ("row", "layer"))
    weights = jnp.dot(
        upper, projection, precision=lax.Precision.HIGHEST, preferred_element_type=jnp.float32
    )
    return data - jnp.dot(
        panel_vectors, weights, precision=lax.Precision.HIGHEST, preferred_element_type=jnp.float32
    )


def on_device(
    eigvecs,
    first_vectors,
    second_vectors,
    first_factors,
    second_factors,
    panel_vectors,
    panel_factor,
):
    upper = jnp.triu(panel_factor)
    reflectors = (
        lax.all_gather(first_vectors, "col", axis=1, tiled=True),
        lax.all_gather(second_vectors, "col", axis=1, tiled=True),
        lax.all_gather(first_factors, "col", axis=1, tiled=True),
        lax.all_gather(second_factors, "col", axis=1, tiled=True),
    )
    tiles = to_tiles(eigvecs)
    tiles = band_tile(tiles, reflectors[0], reflectors[1], reflectors[2], reflectors[3])
    return panel_tile(tiles, panel_vectors, upper)


def solution(mesh):
    in_specs = (
        P("row", ("col", "layer")),
        P(("row", "layer"), "col"),
        P(("row", "layer"), "col"),
        P(("row", "layer"), "col"),
        P(("row", "layer"), "col"),
        P(("row", "layer"), None),
        P(),
    )
    out_specs = P(("row", "layer"), "col")
    return jax.shard_map(
        on_device, mesh=mesh, in_specs=in_specs, out_specs=out_specs, check_vma=False
    )
```

profile of v0, /device:TPU:0, one launch (start us, length us, event | category | flops | bytes accessed | tf_op | source)
XLA Modules:
  0.0 561.3 jit_solution(13967101943740955004)
XLA Ops:
  6.5 7.1 %all-to-all-start = ((f32[4,2048,512]{2,1,0:T(8,128)}), f32[4,2048,512]{2,1,0:T(8,128)}, u32[]{:S(2)}, u32[]{:S(2)}) async-start(f32[4,2048,512]{2,1,0:T(8,128)} %bitcast.38), calls=%async_computation | async-start | bytes 33554432 | tf_op jit(solution)/shard_map/all_to_all | solution.py:61
  13.7 0.0 all-gather.3.cloned.1.call-start
  13.7 0.7 all-gather.3.cloned.1.call-update
  14.4 0.0 all-gather.5.cloned.1.call-start
  14.4 0.7 all-gather.5.cloned.1.call-update
  15.1 0.0 all-reduce.2.cloned.1.call-start
  15.2 0.0 copy-done.6
  15.2 20.1 %all_gather.12 = f32[1024,128]{0,1:T(8,128)S(1)} all-gather(f32[1024,32]{0,1:T(8,128)S(1)} %copy-done.6), channel_id=1, replica_groups=mesh['row'=2,'col'=4,'layer'=4] {'col'}, dimensions={1}, use_global_device_ids=true | all-gather | bytes 655360 | tf_op jit(solution)/shard_map/all_gather | solution.py:90
  35.3 1.0 copy.51
  36.4 0.1 iota_compare_fusion.2
  36.5 13.3 %all-gather.3.cloned.1.call-done = f32[2048,128]{0,1:T(8,128)} async-done(((f32[2048,32]{0,1:T(8,128)}), f32[2048,128]{0,1:T(8,128)}) %all-gather.3.cloned.1.call-update) | async-done | bytes 1048592 | tf_op jit(solution)/shard_map/all_gather | solution.py:88
  49.8 2.6 copy.41
  52.4 26.1 %all-gather.5.cloned.1.call-done = f32[2048,128]{0,1:T(8,128)} async-done(((f32[2048,32]{0,1:T(8,128)}), f32[2048,128]{0,1:T(8,128)}) %all-gather.5.cloned.1.call-update) | async-done | bytes 1048592 | tf_op jit(solution)/shard_map/all_gather | solution.py:89
  78.5 1.5 copy.43
  80.1 117.2 %all-to-all-done = f32[4,2048,512]{2,1,0:T(8,128)} async-done(((f32[4,2048,512]{2,1,0:T(8,128)}), f32[4,2048,512]{2,1,0:T(8,128)}, u32[]{:S(2)}, u32[]{:S(2)}) %all-to-all-start) | async-done | bytes 16777248 | tf_op jit(solution)/shard_map/all_to_all | solution.py:61
  197.3 20.9 %copy.39 = f32[2048,4,512]{2,1,0:T(4,128)} copy(f32[2048,4,512]{2,0,1:T(8,128)} %bitcast.1) | data formatting | bytes 33554432 | tf_op jit(solution)/shard_map/all_to_all | solution.py:61
  218.2 20.5 %reshape.28 = f32[8,256,2048]{2,1,0:T(8,128)} reshape(f32[2048,4,512]{2,1,0:T(4,128)} %copy.39) | data formatting | bytes 33554432 | tf_op jit(solution)/shard_map/reshape | solution.py:29
  238.8 14.5 %fusion.16 = f32[8,128,2048]{2,1,0:T(8,128)S(1)} fusion(f32[8,256,128]{2,1,0:T(8,128)} %bitcast.41, f32[8,256,2048]{2,1,0:T(8,128)} %reshape.28), kind=kOutput, calls=%fused_computation.29 | convolution fusion | flops 6442450944 | bytes 26214400 | tf_op jit(solution)/shard_map/kri,krc->kic/dot_general | solution.py:32
  253.3 0.0 copy-done.4
  253.3 9.6 %fusion.2 = f32[8,128,2048]{2,1,0:T(8,128)} fusion(f32[8,128,2048]{2,1,0:T(8,128)S(1)} %fusion.16, f32[8,128,128]{2,1,0:T(8,128)S(1)} %bitcast.44, pred[128,128]{1,0:T(8,128)(4,1)S(1)} %iota_compare_fusion.2), kind=kOutput, calls=%fused_computation.11 | convolution fusion | flops 3221356544 | bytes 17317888 | tf_op jit(solution)/shard_map/kij,kjc->kic/dot_general | solution.py:33
  262.9 22.4 %bitcast_subtract_fusion.1 = f32[8,256,2048]{2,1,0:T(8,128)} fusion(f32[8,256,2048]{2,1,0:T(8,128)} %reshape.28, f32[8,128,2048]{2,1,0:T(8,128)} %fusion.2, f32[8,256,128]{2,1,0:T(8,128)S(1)} %bitcast.42), kind=kOutput, calls=%fused_computation.2 | convolution fusion | flops 6446645248 | bytes 42991616 | tf_op jit(solution)/shard_map/kri,kic->krc/dot_general | solution.py:34
  285.4 3.1 pad_maximum_fusion.3
  288.5 2.3 collective-permute-start
  290.8 1.3 collective-permute-start.1
  292.1 18.3 %all_gather.15 = f32[1024,128]{0,1:T(8,128)} all-gather(f32[1024,32]{0,1:T(8,128)S(1)} %copy-done.7), channel_id=1, replica_groups=mesh['row'=2,'col'=4,'layer'=4] {'col'}, dimensions={1}, use_global_device_ids=true | all-gather | bytes 655360 | tf_op jit(solution)/shard_map/all_gather | solution.py:91
  310.3 2.0 copy.45
  312.4 0.8 slice.25
  313.2 1.3 collective-permute-start.2
  314.5 1.8 collective-permute-done.2
  316.4 1.9 pad_maximum_fusion.4
  318.3 0.0 collective-permute-done
  318.3 0.0 collective-permute-done.1
  318.3 0.0 slice-start.1
  318.3 0.0 slice-start.2
  318.3 19.1 %pad_maximum_fusion = f32[2304,2176]{1,0:T(8,128)} fusion(f32[128,2176]{1,0:T(8,128)} %collective-permute-done.1, f32[2048,128]{1,0:T(8,128)S(1)} %copy.43, f32[2048,2048]{1,0:T(8,128)} %bitcast.30, f32[128,2176]{1,0:T(8,128)} %collective-permute-done), kind=kLoop, calls=%fused_computation | loop fusion | flops 15040512 | bytes 40108032 | tf_op jit(solution)/shard_map/concatenate | solution.py:16
  337.4 15.5 %slice.24 = f32[2304,2048]{1,0:T(8,128)} slice(f32[2304,2176]{1,0:T(8,128)} %pad_maximum_fusion), slice={[0:2304], [0:2048]} | slice | bytes 37748736 | tf_op jit(solution)/shard_map/slice | solution.py:45
  352.9 1.0 pad_maximum_fusion.1
  353.9 14.0 %fusion.17 = f32[9,128,2048]{2,1,0:T(8,128)S(1)} fusion(f32[9,256,128]{2,1,0:T(8,128)S(1)} %bitcast.39, f32[9,256,2048]{2,1,0:T(8,128)} %bitcast.34), kind=kOutput, calls=%fused_computation.30 | convolution fusion | flops 7247757312 | bytes 29491200 | tf_op jit(solution)/shard_map/kri,krc->kic/dot_general | solution.py:32
  367.9 11.8 %fusion = f32[9,128,2048]{2,1,0:T(8,128)} fusion(f32[9,128,2048]{2,1,0:T(8,128)S(1)} %fusion.17, f32[9,128,128]{2,1,0:T(8,128)} %bitcast.43, pred[128,128]{1,0:T(8,128)(4,1)S(1)} %iota_compare_fusion.2), kind=kOutput, calls=%fused_computation.9 | convolution fusion | flops 3624026112 | bytes 19480576 | tf_op jit(solution)/shard_map/kij,kjc->kic/dot_general | solution.py:33
  379.7 25.0 %convolution_subtract_fusion = f32[9,256,2048]{2,1,0:T(8,128)} fusion(f32[9,256,2048]{2,1,0:T(8,128)} %bitcast.35, f32[9,256,128]{2,1,0:T(8,128)S(1)} %bitcast.40, f32[9,128,2048]{2,1,0:T(8,128)} %fusion), kind=kOutput, calls=%fused_computation.3 | convolution fusion | flops 7252475904 | bytes 48365568 | tf_op jit(solution)/shard_map/kri,kic->krc/dot_general | solution.py:34
  404.7 29.7 %convolution_bitcast_fusion = f32[256,2048]{0,1:T(8,128)} fusion(f32[2048,256]{1,0:T(8,128)S(1)} %copy-done, f32[2304,2048]{1,0:T(8,128)} %bitcast.36), kind=kOutput, calls=%fused_computation.4 | convolution fusion | flops 12884901888 | bytes 20971520 | tf_op jit(solution)/shard_map/dot_general | solution.py:65
  434.4 0.0 all-reduce.2.cloned.1.call-update
  434.5 11.8 %slice.26 = f32[2048,2048]{1,0:T(8,128)} slice(f32[2304,2048]{1,0:T(8,128)} %bitcast.37), slice={[128:2176], [0:2048]} | slice | bytes 33554432
  446.3 18.2 %copy.52 = f32[2048,2048]{0,1:T(8,128)} copy(f32[2048,2048]{1,0:T(8,128)} %slice.26) | data formatting | bytes 33554432
  464.5 35.2 %all-reduce.2.cloned.1.call-done = f32[256,2048]{0,1:T(8,128)} async-done(((f32[256,2048]{0,1:T(8,128)}), f32[256,2048]{0,1:T(8,128)}) %all-reduce.2.cloned.1.call-update) | async-done | bytes 2097168 | tf_op jit(solution)/shard_map/psum | solution.py:68
  499.7 3.5 fusion.6
  503.3 33.4 %bitcast_subtract_fusion = f32[2048,2048]{0,1:T(8,128)} fusion(f32[2048,2048]{0,1:T(8,128)} %copy.52, f32[256,2048]{1,0:T(8,128)S(1)} %fusion.6, f32[2048,256]{1,0:T(8,128)S(1)} %copy-done), kind=kOutput, calls=%fused_computation.1 | convolution fusion | flops 12889096192 | bytes 37748736 | tf_op jit(solution)/shard_map/dot_general | solution.py:72
  536.7 17.6 %copy.48 = f32[2048,2048]{1,0:T(8,128)} copy(f32[2048,2048]{0,1:T(8,128)} %bitcast_subtract_fusion) | data formatting | bytes 33554432 | tf_op jit(solution)/shard_map/sub | solution.py:72
  (23 shorter events, 0.0 us)
Async XLA Ops:
  6.5 398.2 %copy-start = (f32[2048,256]{1,0:T(8,128)S(1)}, f32[2048,256]{1,0:T(8,128)}, u32[]{:S(2)}) copy-start(f32[2048,256]{1,0:T(8,128)} %param.12) | copy-start | bytes 6291460
  6.5 8.7 %copy-start.6 = (f32[1024,32]{0,1:T(8,128)S(1)}, f32[1024,32]{0,1:T(8,128)}, u32[]{:S(2)}) copy-start(f32[1024,32]{0,1:T(8,128)} %param.10) | copy-start | bytes 393220
  6.5 190.8 %all-to-all-start = ((f32[4,2048,512]{2,1,0:T(8,128)}), f32[4,2048,512]{2,1,0:T(8,128)}, u32[]{:S(2)}, u32[]{:S(2)}) async-start(f32[4,2048,512]{2,1,0:T(8,128)} %bitcast.38), calls=%async_computation | async-start | bytes 33554432 | tf_op jit(solution)/shard_map/all_to_all | solution.py:61
  13.7 36.1 %all-gather.3.cloned.1.call-start = ((), (), s32[]{:S(2)}) async-start(), calls=%async_computation.1 | async-start | bytes 1310720 | tf_op jit(solution)/shard_map/all_gather | solution.py:88
  14.4 64.1 %all-gather.5.cloned.1.call-start = ((), (), s32[]{:S(2)}) async-start(), calls=%async_computation.2 | async-start | bytes 1310720 | tf_op jit(solution)/shard_map/all_gather | solution.py:89
  15.1 484.6 %all-reduce.2.cloned.1.call-start = ((), (), s32[]{:S(2)}) async-start(), calls=%async_computation.3 | async-start | bytes 4194304 | tf_op jit(solution)/shard_map/psum | solution.py:68
  238.8 14.5 %copy-start.4 = (f32[1024,128]{1,0:T(8,128)S(1)}, f32[1024,128]{1,0:T(8,128)}, u32[]{:S(2)}) copy-start(f32[1024,128]{1,0:T(8,128)} %copy.51) | copy-start | bytes 1572868
  253.3 9.6 %copy-start.3 = (f32[2048,128]{1,0:T(8,128)S(1)}, f32[2048,128]{1,0:T(8,128)}, u32[]{:S(2)}) copy-start(f32[2048,128]{1,0:T(8,128)} %copy.41) | copy-start | bytes 3145732
  285.4 6.7 %copy-start.7 = (f32[1024,32]{0,1:T(8,128)S(1)}, f32[1024,32]{0,1:T(8,128)}, u32[]{:S(2)}) copy-start(f32[1024,32]{0,1:T(8,128)} %param.11) | copy-start | bytes 393220
  288.5 29.8 %collective-permute-start = (f32[128,2176]{1,0:T(8,128)}, f32[128,2176]{1,0:T(8,128)}, u32[]{:S(2)}, u32[]{:S(2)}) collective-permute-start(f32[128,2176]{1,0:T(8,128)} %get-tuple-element.5), channel_id=1, source_target_pairs={{0,1},{1,2},{2,3},{3,16},{16,17},{17,18},{18,19},{4,5},{5,6},{6,7}... | collective-permute-start | bytes 3342344 | tf_op jit(solution)/shard_map/ppermute | solution.py:14
  290.8 27.5 %collective-permute-start.1 = (f32[128,2176]{1,0:T(8,128)}, f32[128,2176]{1,0:T(8,128)}, u32[]{:S(2)}, u32[]{:S(2)}) collective-permute-start(f32[128,2176]{1,0:T(8,128)} %get-tuple-element.6), channel_id=1, source_target_pairs={{1,0},{2,1},{3,2},{16,3},{17,16},{18,17},{19,18},{5,4},{6,5},{7,6}... | collective-permute-start | bytes 3342344 | tf_op jit(solution)/shard_map/ppermute | solution.py:15
  313.2 3.1 collective-permute-start.2
  318.3 34.6 %slice-start = ((s8[16777216]{0:T(1024)(128)(4,1)}), s8[4194304]{0:T(1024)(128)(4,1)S(1)}, s32[]{:S(2)}) async-start(s8[16777216]{0:T(1024)(128)(4,1)} %bitcast.31), calls=%async_computation.4 | async-start | bytes 8388608
  318.3 34.6 %slice-start.1 = ((s8[16777216]{0:T(1024)(128)(4,1)}), s8[4194304]{0:T(1024)(128)(4,1)S(1)}, s32[]{:S(2)}) async-start(s8[16777216]{0:T(1024)(128)(4,1)} %bitcast.31), calls=%async_computation.5 | async-start | bytes 8388608
  318.3 34.6 %slice-start.2 = ((s8[16777216]{0:T(1024)(128)(4,1)}), s8[4194304]{0:T(1024)(128)(4,1)S(1)}, s32[]{:S(2)}) async-start(s8[16777216]{0:T(1024)(128)(4,1)} %bitcast.31), calls=%async_computation.6 | async-start | bytes 8388608
  337.4 15.5 %slice-start.3 = ((s8[16777216]{0:T(1024)(128)(4,1)}), s8[4194304]{0:T(1024)(128)(4,1)S(1)}, s32[]{:S(2)}) async-start(s8[16777216]{0:T(1024)(128)(4,1)} %bitcast.31), calls=%async_computation.7 | async-start | bytes 8388608
  353.9 14.0 %copy-start.1 = (f32[2304,128]{1,0:T(8,128)}, f32[2304,128]{1,0:T(8,128)S(1)}, u32[]{:S(2)}) copy-start(f32[2304,128]{1,0:T(8,128)S(1)} %pad_maximum_fusion.1) | copy-start | bytes 3538948
  367.9 11.9 %copy-start.2 = (f32[2304,128]{1,0:T(8,128)S(1)}, f32[2304,128]{1,0:T(8,128)}, u32[]{:S(2)}) copy-start(f32[2304,128]{1,0:T(8,128)} %copy-done.1) | copy-start | bytes 3538948
  446.3 53.5 %copy-start.5 = (f32[256,256]{1,0:T(8,128)S(1)}, f32[256,256]{1,0:T(8,128)}, u32[]{:S(2)}) copy-start(f32[256,256]{1,0:T(8,128)} %param.13) | copy-start | bytes 786436
Sparse Core Ops, SparseCore 0:
  16.0 33.7 all-gather.2
  51.4 27.1 all-gather.4
  434.6 65.1 all-reduce.1
where the time goes:
time: 572 us; the launch traced here: 561 us
  waiting for transfers between devices  195 us (34%)
  matrix products  164 us (29%)
  local copies, waits for them, and re-layouts  113 us (20%)
  blocking collectives  38.4 us (7%)
  other arithmetic  25.2 us (4%)
  between operations  13.7 us (2%)
  starting transfers between devices  12.1 us (2%)
    all_to_all x1, waiting for transfers between devices, to_tiles(): lax.all_to_all(data, 'layer', split_axis=0, concat_axis=1, tiled=True)  117 us
    dot_general x2, matrix products, apply_windows(): jnp.einsum('kri,kic->krc', vec_blocks, scaled, precision=lax.Precision.HI...  47.4 us
    psum x1, waiting for transfers between devices, panel_tile(): projection = lax.psum(partial_value, ('row', 'layer'))  35.2 us
    dot_general x1, matrix products, panel_tile(): jnp.dot(panel_vectors, weights, precision=lax.Precision.HIGHEST, preferre...  33.4 us
    unnamed x26, local copies, waits for them, and re-layouts  30.1 us
    dot_general x1, matrix products, panel_tile(): jnp.dot(panel_vectors.T, data, precision=lax.Precision.HIGHEST, preferred...  29.7 us
    dot_general x2, matrix products, apply_windows(): jnp.einsum('kri,krc->kic', vec_blocks, blocks, precision=lax.Precision.HI...  28.5 us
    all_gather x1, waiting for transfers between devices, on_device(): lax.all_gather(second_vectors, 'col', axis=1, tiled=True)  26.1 us
  transfers between devices with their start and end apart: 7, of which 5 were waited for; matrix products, arithmetic and copies ran while one was open for 7% of the time, Pallas kernels for 0%

commit v1 on v0

--- a/solution.py
+++ b/solution.py
@@ -58,7 +58,10 @@
 
 
 def to_tiles(data):
-    return lax.all_to_all(data, "layer", split_axis=0, concat_axis=1, tiled=True)
+    return jnp.concatenate(
+        lax.all_to_all(jnp.stack(jnp.split(data, lax.axis_size("layer"), axis=0)), "layer", 0, 0),
+        axis=1,
+    )
 
 
 def panel_tile(data, panel_vectors, upper):

time: 572 us -> 600 us (1.049)
  matrix products: 164 us -> 179 us
  other arithmetic: 25.2 us -> 31.6 us
  local copies, waits for them, and re-layouts: 113 us -> 119 us
    another operation x0 -> x3, local copies, waits for them, and re-layouts: none -> 48.5 us  [the longest x2 41.4 us: apply_windows(): blocks = data.reshape(count, 256, width)]
    all_to_all x1 -> x0, local copies, waits for them, and re-layouts: 20.9 us -> none  [to_tiles(): lax.all_to_all(data, 'layer', split_axis=0, concat_axis=1, tiled=True)]
    reshape x1 -> x0, local copies, waits for them, and re-layouts: 20.5 us -> none  [apply_windows(): blocks = data.reshape(count, 256, width)]
    dot_general x2, matrix products: 28.5 us -> 43.7 us  [apply_windows(): jnp.einsum('kri,krc->kic', vec_blocks, blocks, precision=lax.Precision.HI...]
    another operation x0 -> x1, other arithmetic: none -> 6.38 us  [to_tiles(): jnp.stack(jnp.split(data, lax.axis_size('layer'), axis=0))]
where the time goes in v1:
time: 600 us; the launch traced here: 590 us
  waiting for transfers between devices  195 us (32%)
  matrix products  179 us (30%)
  local copies, waits for them, and re-layouts  119 us (20%)
  blocking collectives  38.4 us (6%)
  other arithmetic  31.6 us (5%)
  between operations  13.5 us (2%)
  starting transfers between devices  12.1 us (2%)
    all_to_all x1, waiting for transfers between devices, to_tiles(): lax.all_to_all(jnp.stack(jnp.split(data, lax.axis_size('layer'), axis=0))...  117 us
    dot_general x2, matrix products, apply_windows(): jnp.einsum('kri,kic->krc', vec_blocks, scaled, precision=lax.Precision.HI...  47.4 us
    dot_general x2, matrix products, apply_windows(): jnp.einsum('kri,krc->kic', vec_blocks, blocks, precision=lax.Precision.HI...  43.7 us
    another operation x2, local copies, waits for them, and re-layouts, apply_windows(): blocks = data.reshape(count, 256, width)  41.4 us
    psum x1, waiting for transfers between devices, panel_tile(): projection = lax.psum(partial_value, ('row', 'layer'))  35.4 us
    dot_general x1, matrix products, panel_tile(): jnp.dot(panel_vectors, weights, precision=lax.Precision.HIGHEST, preferre...  33.3 us
    unnamed x26, local copies, waits for them, and re-layouts  29.9 us
    dot_general x1, matrix products, panel_tile(): jnp.dot(panel_vectors.T, data, precision=lax.Precision.HIGHEST, preferred...  29.7 us
  transfers between devices with their start and end apart: 7, of which 5 were waited for; matrix products, arithmetic and copies ran while one was open for 7% of the time, Pallas kernels for 0%

profile of v1, /device:TPU:0, one launch (start us, length us, event | category | flops | bytes accessed | tf_op | source)
XLA Modules:
  0.0 589.7 jit_solution(11896225304437344640)
XLA Ops:
  6.5 7.0 %slice_bitcast_fusion.3 = (f32[1,2048,512]{2,1,0:T(8,128)S(1)}, f32[1,2048,512]{2,1,0:T(8,128)S(1)}, f32[1,2048,512]{2,1,0:T(8,128)S(1)}, f32[1,2048,512]{2,1,0:T(8,128)S(1)}) fusion(f32[8192,512]{1,0:T(8,128)} %param.7), kind=kLoop, calls=%fused_computation.8 | loop fusion | bytes 33554432 | tf_op jit(solution)/shard_map/stack | solution.py:62
  13.6 6.4 %pad_maximum_fusion.1 = f32[4,2048,512]{2,1,0:T(8,128)} fusion(f32[1,2048,512]{2,1,0:T(8,128)S(1)} %get-tuple-element.9, f32[1,2048,512]{2,1,0:T(8,128)S(1)} %get-tuple-element.10, f32[1,2048,512]{2,1,0:T(8,128)S(1)} %get-tuple-element.8, f32[1,2048,512]{2,1,0:T(8,128)S(1)} %get-tuple-element.7), kind=kLoop, calls=%fused_computation.1 | loop fusion | flops 12582912 | bytes 33554432 | tf_op jit(solution)/shard_map/stack | solution.py:62
  20.0 7.1 %all-to-all-start = ((f32[4,2048,512]{2,1,0:T(8,128)}), f32[4,2048,512]{2,1,0:T(8,128)}, u32[]{:S(2)}, u32[]{:S(2)}) async-start(f32[4,2048,512]{2,1,0:T(8,128)} %pad_maximum_fusion.1), calls=%async_computation | async-start | bytes 33554432 | tf_op jit(solution)/shard_map/all_to_all | solution.py:62
  27.1 0.0 all-gather.3.cloned.1.call-start
  27.1 0.7 all-gather.3.cloned.1.call-update
  27.8 0.0 all-gather.5.cloned.1.call-start
  27.9 0.7 all-gather.5.cloned.1.call-update
  28.6 0.0 all-reduce.2.cloned.1.call-start
  28.6 20.1 %all_gather.12 = f32[1024,128]{0,1:T(8,128)S(1)} all-gather(f32[1024,32]{0,1:T(8,128)S(1)} %copy-done.6), channel_id=1, replica_groups=mesh['row'=2,'col'=4,'layer'=4] {'col'}, dimensions={1}, use_global_device_ids=true | all-gather | bytes 655360 | tf_op jit(solution)/shard_map/all_gather | solution.py:93
  48.8 1.0 copy.52
  49.8 0.1 iota_compare_fusion.2
  49.9 13.4 %all-gather.3.cloned.1.call-done = f32[2048,128]{0,1:T(8,128)} async-done(((f32[2048,32]{0,1:T(8,128)}), f32[2048,128]{0,1:T(8,128)}) %all-gather.3.cloned.1.call-update) | async-done | bytes 1048592 | tf_op jit(solution)/shard_map/all_gather | solution.py:91
  63.2 2.6 copy.42
  65.9 26.1 %all-gather.5.cloned.1.call-done = f32[2048,128]{0,1:T(8,128)} async-done(((f32[2048,32]{0,1:T(8,128)}), f32[2048,128]{0,1:T(8,128)}) %all-gather.5.cloned.1.call-update) | async-done | bytes 1048592 | tf_op jit(solution)/shard_map/all_gather | solution.py:92
  92.0 1.5 copy.45
  93.5 117.2 %all-to-all-done = f32[4,2048,512]{2,1,0:T(8,128)} async-done(((f32[4,2048,512]{2,1,0:T(8,128)}), f32[4,2048,512]{2,1,0:T(8,128)}, u32[]{:S(2)}, u32[]{:S(2)}) %all-to-all-start) | async-done | bytes 16777248 | tf_op jit(solution)/shard_map/all_to_all | solution.py:62
  210.8 20.9 %copy.54 = f32[2048,4,512]{2,1,0:T(4,128)} copy(f32[2048,4,512]{2,0,1:T(8,128)} %bitcast.4) | data formatting | bytes 33554432 | tf_op jit(solution)/shard_map/reshape;reshape | solution.py:29
  231.7 20.5 %reshape.32 = f32[8,256,2048]{2,1,0:T(8,128)} reshape(f32[2048,4,512]{2,1,0:T(4,128)} %copy.54) | data formatting | bytes 33554432 | tf_op jit(solution)/shard_map/reshape;reshape | solution.py:29
  252.2 29.7 %fusion.16 = f32[8,2048,128]{2,1,0:T(8,128)S(1)} fusion(f32[8,256,2048]{2,1,0:T(8,128)} %reshape.32, f32[8,256,128]{2,1,0:T(8,128)} %bitcast.47), kind=kOutput, calls=%fused_computation.34 | convolution fusion | flops 6442450944 | bytes 26214400 | tf_op jit(solution)/shard_map/kri,krc->kic/dot_general | solution.py:32
  282.0 9.8 %fusion.2 = f32[8,128,2048]{2,1,0:T(8,128)} fusion(f32[8,2048,128]{2,1,0:T(8,128)S(1)} %fusion.16, f32[8,128,128]{2,1,0:T(8,128)S(1)} %bitcast.50, pred[128,128]{1,0:T(8,128)(4,1)S(1)} %iota_compare_fusion.2), kind=kOutput, calls=%fused_computation.16 | convolution fusion | flops 3221356544 | bytes 17317888 | tf_op jit(solution)/shard_map/kij,kjc->kic/dot_general | solution.py:33
  291.7 22.3 %bitcast_subtract_fusion.1 = f32[8,256,2048]{2,1,0:T(8,128)} fusion(f32[8,256,2048]{2,1,0:T(8,128)} %reshape.32, f32[8,128,2048]{2,1,0:T(8,128)} %fusion.2, f32[8,256,128]{2,1,0:T(8,128)S(1)} %bitcast.48), kind=kOutput, calls=%fused_computation.3 | convolution fusion | flops 6446645248 | bytes 42991616 | tf_op jit(solution)/shard_map/kri,kic->krc/dot_general | solution.py:34
  314.0 3.1 pad_maximum_fusion.4
  317.2 2.3 collective-permute-start
  319.4 1.3 collective-permute-start.1
  320.7 18.3 %all_gather.15 = f32[1024,128]{0,1:T(8,128)} all-gather(f32[1024,32]{0,1:T(8,128)S(1)} %copy-done.7), channel_id=1, replica_groups=mesh['row'=2,'col'=4,'layer'=4] {'col'}, dimensions={1}, use_global_device_ids=true | all-gather | bytes 655360 | tf_op jit(solution)/shard_map/all_gather | solution.py:94
  339.0 2.0 copy.47
  341.1 0.8 slice.25
  341.9 1.3 collective-permute-start.2
  343.2 1.8 collective-permute-done.2
  345.1 1.9 pad_maximum_fusion.5
  347.0 0.0 collective-permute-done
  347.0 0.0 collective-permute-done.1
  347.0 0.0 slice-start.1
  347.0 0.0 slice-start.2
  347.0 19.1 %pad_maximum_fusion = f32[2304,2176]{1,0:T(8,128)} fusion(f32[128,2176]{1,0:T(8,128)} %collective-permute-done.1, f32[2048,128]{1,0:T(8,128)S(1)} %copy.45, f32[2048,2048]{1,0:T(8,128)} %bitcast.37, f32[128,2176]{1,0:T(8,128)} %collective-permute-done), kind=kLoop, calls=%fused_computation | loop fusion | flops 15040512 | bytes 40108032 | tf_op jit(solution)/shard_map/concatenate | solution.py:16
  366.1 15.5 %slice.24 = f32[2304,2048]{1,0:T(8,128)} slice(f32[2304,2176]{1,0:T(8,128)} %pad_maximum_fusion), slice={[0:2304], [0:2048]} | slice | bytes 37748736 | tf_op jit(solution)/shard_map/slice | solution.py:45
  381.6 1.0 pad_maximum_fusion.2
  382.6 14.0 %fusion.17 = f32[9,128,2048]{2,1,0:T(8,128)S(1)} fusion(f32[9,256,128]{2,1,0:T(8,128)S(1)} %bitcast.45, f32[9,256,2048]{2,1,0:T(8,128)} %bitcast.41), kind=kOutput, calls=%fused_computation.35 | convolution fusion | flops 7247757312 | bytes 29491200 | tf_op jit(solution)/shard_map/kri,krc->kic/dot_general | solution.py:32
  396.6 11.8 %fusion = f32[9,128,2048]{2,1,0:T(8,128)} fusion(f32[9,128,2048]{2,1,0:T(8,128)S(1)} %fusion.17, f32[9,128,128]{2,1,0:T(8,128)} %bitcast.49, pred[128,128]{1,0:T(8,128)(4,1)S(1)} %iota_compare_fusion.2), kind=kOutput, calls=%fused_computation.14 | convolution fusion | flops 3624026112 | bytes 19480576 | tf_op jit(solution)/shard_map/kij,kjc->kic/dot_general | solution.py:33
  408.4 25.1 %convolution_subtract_fusion = f32[9,256,2048]{2,1,0:T(8,128)} fusion(f32[9,256,2048]{2,1,0:T(8,128)} %bitcast.42, f32[9,256,128]{2,1,0:T(8,128)S(1)} %bitcast.46, f32[9,128,2048]{2,1,0:T(8,128)} %fusion), kind=kOutput, calls=%fused_computation.4 | convolution fusion | flops 7252475904 | bytes 48365568 | tf_op jit(solution)/shard_map/kri,kic->krc/dot_general | solution.py:34
  433.6 29.7 %convolution_bitcast_fusion = f32[256,2048]{0,1:T(8,128)} fusion(f32[2048,256]{1,0:T(8,128)S(1)} %copy-done, f32[2304,2048]{1,0:T(8,128)} %bitcast.43), kind=kOutput, calls=%fused_computation.9 | convolution fusion | flops 12884901888 | bytes 20971520 | tf_op jit(solution)/shard_map/dot_general | solution.py:68
  463.3 0.0 all-reduce.2.cloned.1.call-update
  463.3 11.8 %slice.26 = f32[2048,2048]{1,0:T(8,128)} slice(f32[2304,2048]{1,0:T(8,128)} %bitcast.44), slice={[128:2176], [0:2048]} | slice | bytes 33554432
  475.1 18.0 %copy.53 = f32[2048,2048]{0,1:T(8,128)} copy(f32[2048,2048]{1,0:T(8,128)} %slice.26) | data formatting | bytes 33554432
  493.1 35.4 %all-reduce.2.cloned.1.call-done = f32[256,2048]{0,1:T(8,128)} async-done(((f32[256,2048]{0,1:T(8,128)}), f32[256,2048]{0,1:T(8,128)}) %all-reduce.2.cloned.1.call-update) | async-done | bytes 2097168 | tf_op jit(solution)/shard_map/psum | solution.py:71
  528.6 3.5 fusion.6
  532.1 33.3 %bitcast_subtract_fusion = f32[2048,2048]{0,1:T(8,128)} fusion(f32[2048,2048]{0,1:T(8,128)} %copy.53, f32[256,2048]{1,0:T(8,128)S(1)} %fusion.6, f32[2048,256]{1,0:T(8,128)S(1)} %copy-done), kind=kOutput, calls=%fused_computation.2 | convolution fusion | flops 12889096192 | bytes 37748736 | tf_op jit(solution)/shard_map/dot_general | solution.py:75
  565.3 17.6 %copy.50 = f32[2048,2048]{1,0:T(8,128)} copy(f32[2048,2048]{0,1:T(8,128)} %bitcast_subtract_fusion) | data formatting | bytes 33554432 | tf_op jit(solution)/shard_map/sub | solution.py:75
  (25 shorter events, 0.1 us)
Async XLA Ops:
  6.5 427.0 %copy-start = (f32[2048,256]{1,0:T(8,128)S(1)}, f32[2048,256]{1,0:T(8,128)}, u32[]{:S(2)}) copy-start(f32[2048,256]{1,0:T(8,128)} %param.12) | copy-start | bytes 6291460
  20.0 8.7 %copy-start.6 = (f32[1024,32]{0,1:T(8,128)S(1)}, f32[1024,32]{0,1:T(8,128)}, u32[]{:S(2)}) copy-start(f32[1024,32]{0,1:T(8,128)} %param.10) | copy-start | bytes 393220
  20.0 190.8 %all-to-all-start = ((f32[4,2048,512]{2,1,0:T(8,128)}), f32[4,2048,512]{2,1,0:T(8,128)}, u32[]{:S(2)}, u32[]{:S(2)}) async-start(f32[4,2048,512]{2,1,0:T(8,128)} %pad_maximum_fusion.1), calls=%async_computation | async-start | bytes 33554432 | tf_op jit(solution)/shard_map/all_to_all | solution.py:62
  27.1 36.1 %all-gather.3.cloned.1.call-start = ((), (), s32[]{:S(2)}) async-start(), calls=%async_computation.1 | async-start | bytes 1310720 | tf_op jit(solution)/shard_map/all_gather | solution.py:91
  27.8 64.1 %all-gather.5.cloned.1.call-start = ((), (), s32[]{:S(2)}) async-start(), calls=%async_computation.2 | async-start | bytes 1310720 | tf_op jit(solution)/shard_map/all_gather | solution.py:92
  28.6 500.0 %all-reduce.2.cloned.1.call-start = ((), (), s32[]{:S(2)}) async-start(), calls=%async_computation.3 | async-start | bytes 4194304 | tf_op jit(solution)/shard_map/psum | solution.py:71
  252.2 29.8 %copy-start.4 = (f32[1024,128]{1,0:T(8,128)S(1)}, f32[1024,128]{1,0:T(8,128)}, u32[]{:S(2)}) copy-start(f32[1024,128]{1,0:T(8,128)} %copy.52) | copy-start | bytes 1572868
  281.9 9.8 %copy-start.3 = (f32[2048,128]{1,0:T(8,128)S(1)}, f32[2048,128]{1,0:T(8,128)}, u32[]{:S(2)}) copy-start(f32[2048,128]{1,0:T(8,128)} %copy.42) | copy-start | bytes 3145732
  314.0 6.7 %copy-start.7 = (f32[1024,32]{0,1:T(8,128)S(1)}, f32[1024,32]{0,1:T(8,128)}, u32[]{:S(2)}) copy-start(f32[1024,32]{0,1:T(8,128)} %param.11) | copy-start | bytes 393220
  317.2 29.8 %collective-permute-start = (f32[128,2176]{1,0:T(8,128)}, f32[128,2176]{1,0:T(8,128)}, u32[]{:S(2)}, u32[]{:S(2)}) collective-permute-start(f32[128,2176]{1,0:T(8,128)} %get-tuple-element.5), channel_id=1, source_target_pairs={{0,1},{1,2},{2,3},{3,16},{16,17},{17,18},{18,19},{4,5},{5,6},{6,7}... | collective-permute-start | bytes 3342344 | tf_op jit(solution)/shard_map/ppermute | solution.py:14
  319.4 27.6 %collective-permute-start.1 = (f32[128,2176]{1,0:T(8,128)}, f32[128,2176]{1,0:T(8,128)}, u32[]{:S(2)}, u32[]{:S(2)}) collective-permute-start(f32[128,2176]{1,0:T(8,128)} %get-tuple-element.6), channel_id=1, source_target_pairs={{1,0},{2,1},{3,2},{16,3},{17,16},{18,17},{19,18},{5,4},{6,5},{7,6}... | collective-permute-start | bytes 3342344 | tf_op jit(solution)/shard_map/ppermute | solution.py:15
  341.9 3.1 collective-permute-start.2
  347.0 34.6 %slice-start = ((s8[16777216]{0:T(1024)(128)(4,1)}), s8[4194304]{0:T(1024)(128)(4,1)S(1)}, s32[]{:S(2)}) async-start(s8[16777216]{0:T(1024)(128)(4,1)} %bitcast.38), calls=%async_computation.4 | async-start | bytes 8388608
  347.0 34.6 %slice-start.1 = ((s8[16777216]{0:T(1024)(128)(4,1)}), s8[4194304]{0:T(1024)(128)(4,1)S(1)}, s32[]{:S(2)}) async-start(s8[16777216]{0:T(1024)(128)(4,1)} %bitcast.38), calls=%async_computation.5 | async-start | bytes 8388608
  347.0 34.6 %slice-start.2 = ((s8[16777216]{0:T(1024)(128)(4,1)}), s8[4194304]{0:T(1024)(128)(4,1)S(1)}, s32[]{:S(2)}) async-start(s8[16777216]{0:T(1024)(128)(4,1)} %bitcast.38), calls=%async_computation.6 | async-start | bytes 8388608
  366.1 15.5 %slice-start.3 = ((s8[16777216]{0:T(1024)(128)(4,1)}), s8[4194304]{0:T(1024)(128)(4,1)S(1)}, s32[]{:S(2)}) async-start(s8[16777216]{0:T(1024)(128)(4,1)} %bitcast.38), calls=%async_computation.7 | async-start | bytes 8388608
  382.6 14.0 %copy-start.1 = (f32[2304,128]{1,0:T(8,128)}, f32[2304,128]{1,0:T(8,128)S(1)}, u32[]{:S(2)}) copy-start(f32[2304,128]{1,0:T(8,128)S(1)} %pad_maximum_fusion.2) | copy-start | bytes 3538948
  396.6 11.9 %copy-start.2 = (f32[2304,128]{1,0:T(8,128)S(1)}, f32[2304,128]{1,0:T(8,128)}, u32[]{:S(2)}) copy-start(f32[2304,128]{1,0:T(8,128)} %copy-done.1) | copy-start | bytes 3538948
  475.1 53.4 %copy-start.5 = (f32[256,256]{1,0:T(8,128)S(1)}, f32[256,256]{1,0:T(8,128)}, u32[]{:S(2)}) copy-start(f32[256,256]{1,0:T(8,128)} %param.13) | copy-start | bytes 786436
Sparse Core Ops, SparseCore 0:
  29.5 33.7 all-gather.2
  64.8 27.1 all-gather.4
  463.4 65.0 all-reduce.1
